TPU v7x, 512 devices: a whole 4x8x8 slice. The times are simulated.
512 devices in a mesh: node: 32 (over z, x_lo, core), local: 16 (over x_hi, y).
Axes of the slice: x: 4 (x_hi: 2, x_lo: 2; x = x_hi * 2 + x_lo), y: 8, z: 8, core: 2. Of those that a mesh axis runs over, the one named last changes fastest.
Arguments:
- tokens: bfloat16 [2048, 4096], P('local', 'node'), may hold values from -6 to 6
- gate_up_codes: bfloat16 [2, 4096, 14336], P(None, 'local', 'node'), may hold values from -127 to 127
- gate_up_scales: bfloat16 [2, 32, 14336], P(None, 'local', 'node'), may hold values from 2.9921532e-05 to 0.00029945374
- d_hidden: bfloat16 [2048, 14336], P('local', 'node'), may hold values from -6 to 6
Outputs:
- hidden: bfloat16 [2048, 14336], P('local', 'node')
- d_tokens: bfloat16 [2048, 4096], P('local', 'node')
- grad_gate_up: float32 [2, 4096, 14336], P(None, 'local', 'node')
All inputs are finite; a program needn't handle non-finite values.
Results may differ from a plain program's by a relative error of at most 0.023.
Values may be sent and summed in bfloat16 or wider, within the bound.
A program may use at most 128 MiB of HBM per device.

v0:
```python
import math
import jax
import jax.numpy as jnp
from jax import lax
from jax.sharding import PartitionSpec as P

BLOCK = 128


def from_everyone(array, axis):
    length = lax.axis_size(axis)
    return lax.all_to_all(
        jnp.broadcast_to(array[None], (length, *array.shape)), axis, 0, 0, tiled=True
    )


def in_order(pieces, dim):
    pieces = jnp.moveaxis(pieces, 0, dim)
    lengths = pieces.shape
    return pieces.reshape(*lengths[:dim], lengths[dim] * lengths[dim + 1], *lengths[dim + 2 :])


def gather_directly(array, axis, dim):
    pieces = from_everyone(array, axis)
    return in_order(pieces, dim)


def cut_along(array, dim, length):
    before, after = (array.shape[:dim], array.shape[dim + 1 :])
    return jnp.moveaxis(array.reshape(*before, length, -1, *after), dim, 0)


def sent_and_summed(array, axis, dim):
    pieces = cut_along(array, dim, lax.axis_size(axis))
    arrived = lax.all_to_all(pieces, axis, split_axis=0, concat_axis=0, tiled=True)
    return arrived.astype(jnp.float32).sum(axis=0)


def sent_together(arrays, axis, dim, along):
    both = jnp.concatenate(arrays, axis=along)
    out, at, outs = (lax.all_gather(both, axis, axis=dim, tiled=True), 0, [])
    for a in arrays:
        outs.append(lax.slice_in_dim(out, at, at + a.shape[along], axis=along))
        at += a.shape[along]
    return tuple(outs)


def dequant(codes, scales):
    shape = codes.shape
    blocked = codes.astype(jnp.float32).reshape(shape[:-2] + (shape[-2] // BLOCK, BLOCK, shape[-1]))
    weight = blocked * scales.astype(jnp.float32)[..., :, None, :]
    return weight.reshape(shape).astype(jnp.bfloat16)


def body(tokens, gate_up_codes, gate_up_scales, d_hidden):
    rows = tokens.shape[0]
    local_count = lax.axis_size("local")
    features = gather_directly(tokens, "node", 1)
    width = features.shape[1]
    all_codes, all_scales = (
        lax.all_gather(gate_up_codes, "local", axis=1, tiled=True),
        lax.all_gather(gate_up_scales, "local", axis=1, tiled=True),
    )
    w_gu = dequant(all_codes, all_scales)
    group = w_gu.shape[2]
    gate = jnp.dot(features, w_gu[0], preferred_element_type=jnp.float32)
    up = jnp.dot(features, w_gu[1], preferred_element_type=jnp.float32)
    sigmoid_gate = jax.nn.sigmoid(gate)
    active = gate * sigmoid_gate
    hidden = (active * up).astype(jnp.bfloat16)
    grad_in = d_hidden.astype(jnp.float32)
    d_gate = (grad_in * up * sigmoid_gate * (1.0 + gate * (1.0 - sigmoid_gate))).astype(
        jnp.bfloat16
    )
    d_up = (grad_in * active).astype(jnp.bfloat16)
    term = lax.dot_general(
        d_gate, w_gu[0], (((1,), (1,)), ((), ())), preferred_element_type=jnp.float32
    )
    term = term + lax.dot_general(
        d_up, w_gu[1], (((1,), (1,)), ((), ())), preferred_element_type=jnp.float32
    )
    rounded = lax.optimization_barrier(term.astype(jnp.bfloat16)).astype(jnp.float32)
    d_tokens = sent_and_summed(rounded.astype(jnp.bfloat16), "node", 1).astype(jnp.bfloat16)
    factor = 1.0 / math.sqrt(rows * local_count)
    owned = width // local_count
    columns = lax.all_to_all(features, "local", split_axis=1, concat_axis=0, tiled=True)
    gate_all, up_all = sent_together((d_gate, d_up), "local", 0, 1)
    both_all = jnp.concatenate(
        [gate_all.reshape(local_count, rows, group), up_all.reshape(local_count, rows, group)],
        axis=2,
    )
    blocks = columns.reshape(local_count, rows, owned)
    numbers = (((1,), (1,)), ((0,), (0,)))
    partial_value = lax.dot_general(
        blocks, both_all, numbers, preferred_element_type=jnp.float32
    ).astype(jnp.bfloat16)
    summed = jnp.sum(partial_value.astype(jnp.float32), axis=0) * factor
    grads = summed.reshape(owned, 2, group).transpose(1, 0, 2)
    return (hidden, d_tokens, grads)


def solution(mesh):
    placed = (
        P("local", "node"),
        P(None, "local", "node"),
        P(None, "local", "node"),
        P("local", "node"),
    )
    return jax.shard_map(
        body,
        mesh=mesh,
        in_specs=placed,
        out_specs=(P("local", "node"), P("local", "node"), P(None, "local", "node")),
        check_vma=False,
    )
```

profile of v0, /device:TPU:8, one launch (start us, length us, event | category | flops | bytes accessed | tf_op | source)
XLA Modules:
  0.0 310.7 jit_solution(12713937167241401182)
XLA Ops:
  7.2 0.0 all-gather.3.cloned.1.call-start
  7.2 0.7 all-gather.3.cloned.1.call-update
  7.9 0.9 copy.25
  8.8 1.3 broadcast_in_dim.2
  10.1 11.6 %all-to-all-start = ((bf16[32,128,128]{1,2,0:T(8,128)(2,1)}), bf16[32,128,128]{1,2,0:T(8,128)(2,1)S(1)}, u32[]{:S(2)}, u32[]{:S(2)}) async-start(bf16[32,128,128]{1,2,0:T(8,128)(2,1)} %broadcast_in_dim.2), calls=%async_computation | async-start | bytes 2097152 | tf_op jit(solution)/shard_map/all_to_all | solution.py:12
  21.7 0.0 all-gather.5.cloned.1.call-start
  21.8 38.0 %all_gather.10 = bf16[2,32,448]{2,0,1:T(2,128)(2,1)S(1)} all-gather(bf16[2,2,448]{2,0,1:T(2,128)(2,1)S(1)} %copy.22), channel_id=1, replica_groups=mesh['node'=32,'local'=16] {'local'}, dimensions={1}, use_global_device_ids=true | all-gather | bytes 60928 | tf_op jit(solution)/shard_map/all_gather | solution.py:62
  59.8 0.2 copy.24
  60.0 7.9 %mul.45 = f32[2,32,128,448]{2,1,3,0:T(8,128)} broadcast(f32[2,32,448]{1,2,0:T(8,128)S(1)} %copy.24), dimensions={0,1,3} | broadcast | bytes 14794752 | tf_op jit(solution)/shard_map/mul | solution.py:51
  67.9 16.0 %mul.46 = f32[2,4096,448]{1,2,0:T(8,128)} reshape(f32[2,32,128,448]{2,1,3,0:T(8,128)} %mul.45) | data formatting | bytes 29360128 | tf_op jit(solution)/shard_map/mul | solution.py:51
  83.8 77.0 %all-gather.3.cloned.1.call-done = bf16[2,4096,448]{1,2,0:T(8,128)(2,1)} async-done(((bf16[2,256,448]{1,2,0:T(8,128)(2,1)}), bf16[2,4096,448]{1,2,0:T(8,128)(2,1)}) %all-gather.3.cloned.1.call-update) | async-done | bytes 7340048 | tf_op jit(solution)/shard_map/all_gather | solution.py:61
  160.9 10.6 %multiply_convert_fusion = bf16[2,4096,448]{1,2,0:T(8,128)(2,1)} fusion(f32[2,4096,448]{1,2,0:T(8,128)} %mul.46, bf16[2,4096,448]{1,2,0:T(8,128)(2,1)} %all-gather.3.cloned.1.call-done), kind=kLoop, calls=%fused_computation.1 | loop fusion | flops 11010048 | bytes 29360128 | tf_op jit(solution)/shard_map/convert_element_type | solution.py:52
  171.5 0.0 all-to-all-done
  171.5 3.3 %fusion.8 = f32[128,448]{0,1:T(8,128)S(1)} fusion(bf16[128,4096]{0,1:T(8,128)(2,1)S(1)} %bitcast.54, bf16[2,4096,448]{1,2,0:T(8,128)(2,1)} %multiply_convert_fusion), kind=kOutput, calls=%fused_computation.17 | convolution fusion | flops 469762048 | bytes 4947968 | tf_op jit(solution)/shard_map/dot_general | solution.py:66
  174.8 0.9 copy-done
  175.7 1.8 fusion.12
  177.5 0.7 pad_maximum_fusion
  178.2 0.0 all-gather.5.cloned.1.call-update
  178.2 2.8 fusion.4
  181.0 2.8 fusion
  183.8 1.3 bitcast_bitcast_fusion
  185.1 7.8 %all-to-all-start.1 = ((bf16[32,128,128]{2,1,0:T(8,128)(2,1)}), bf16[32,128,128]{2,1,0:T(8,128)(2,1)S(1)}, u32[]{:S(2)}, u32[]{:S(2)}) async-start(bf16[32,128,128]{2,1,0:T(8,128)(2,1)} %bitcast_bitcast_fusion), calls=%async_computation.1 | async-start | bytes 2097152 | tf_op jit(solution)/shard_map/all_to_all | solution.py:35
  192.9 1.3 copy.29
  194.2 27.3 %all-to-all-done.1 = bf16[32,128,128]{2,1,0:T(8,128)(2,1)S(1)} async-done(((bf16[32,128,128]{2,1,0:T(8,128)(2,1)}), bf16[32,128,128]{2,1,0:T(8,128)(2,1)S(1)}, u32[]{:S(2)}, u32[]{:S(2)}) %all-to-all-start.1) | async-done | bytes 1048608 | tf_op jit(solution)/shard_map/all_to_all | solution.py:35
  221.5 6.0 %all-to-all-start.2 = ((bf16[128,16,256]{2,0,1:T(8,128)(2,1)}), bf16[128,16,256]{2,0,1:T(8,128)(2,1)S(1)}, u32[]{:S(2)}, u32[]{:S(2)}) async-start(bf16[128,16,256]{2,0,1:T(8,128)(2,1)} %copy.29), calls=%async_computation.2 | async-start | bytes 2097152 | tf_op jit(solution)/shard_map/all_to_all | solution.py:86
  227.5 0.8 reduce_sum.21
  228.3 66.2 %all-gather.5.cloned.1.call-done = bf16[2048,896]{0,1:T(8,128)(2,1)} async-done(((bf16[128,896]{0,1:T(8,128)(2,1)}), bf16[2048,896]{0,1:T(8,128)(2,1)}) %all-gather.5.cloned.1.call-update) | async-done | bytes 3670032 | tf_op jit(solution)/shard_map/all_gather | solution.py:41
  294.5 2.5 slice_bitcast_fusion.7
  297.0 2.2 copy_bitcast_fusion
  299.3 0.0 all-to-all-done.2
  299.3 3.6 %convert_reduce_fusion = f32[896,256]{1,0:T(8,128)S(1)} fusion(bf16[16,128,448]{1,2,0:T(8,128)(2,1)S(1)} %get-tuple-element.8, bf16[16,128,448]{1,2,0:T(8,128)(2,1)} %get-tuple-element.9, bf16[128,16,256]{2,0,1:T(8,128)(2,1)S(1)} %all-to-all-done.2), kind=kOutput, calls=%fused_computation | convolution fusion | flops 957644800 | bytes 5636096 | tf_op jit(solution)/shard_map/dot_general | solution.py:94
  302.9 1.0 broadcast_multiply_fusion
  (7 shorter events, 0.0 us)
Async XLA Ops:
  7.2 14.6 %copy-start.1 = (bf16[2,2,448]{2,1,0:T(2,128)(2,1)S(1)}, bf16[2,2,448]{2,1,0:T(2,128)(2,1)}, u32[]{:S(2)}) copy-start(bf16[2,2,448]{2,1,0:T(2,128)(2,1)} %param.6) | copy-start | bytes 10756
  7.2 153.7 %all-gather.3.cloned.1.call-start = ((), (), s32[]{:S(2)}) async-start(), calls=%async_computation.3 | async-start | bytes 7798784 | tf_op jit(solution)/shard_map/all_gather | solution.py:61
  10.1 161.5 %all-to-all-start = ((bf16[32,128,128]{1,2,0:T(8,128)(2,1)}), bf16[32,128,128]{1,2,0:T(8,128)(2,1)S(1)}, u32[]{:S(2)}, u32[]{:S(2)}) async-start(bf16[32,128,128]{1,2,0:T(8,128)(2,1)} %broadcast_in_dim.2), calls=%async_computation | async-start | bytes 2097152 | tf_op jit(solution)/shard_map/all_to_all | solution.py:12
  21.7 272.8 %all-gather.5.cloned.1.call-start = ((), (), s32[]{:S(2)}) async-start(), calls=%async_computation.4 | async-start | bytes 3899392 | tf_op jit(solution)/shard_map/all_gather | solution.py:41
  160.9 13.9 %copy-start.2 = (bf16[128,448]{0,1:T(8,128)(2,1)S(1)}, bf16[128,448]{0,1:T(8,128)(2,1)}, u32[]{:S(2)}) copy-start(bf16[128,448]{0,1:T(8,128)(2,1)} %param.7) | copy-start | bytes 344068
  171.5 4.2 %copy-start = (bf16[2,4096,448]{1,2,0:T(8,128)(2,1)S(1)}, bf16[2,4096,448]{1,2,0:T(8,128)(2,1)}, u32[]{:S(2)}) copy-start(bf16[2,4096,448]{1,2,0:T(8,128)(2,1)} %multiply_convert_fusion) | copy-start | bytes 22020100
  185.1 36.4 %all-to-all-start.1 = ((bf16[32,128,128]{2,1,0:T(8,128)(2,1)}), bf16[32,128,128]{2,1,0:T(8,128)(2,1)S(1)}, u32[]{:S(2)}, u32[]{:S(2)}) async-start(bf16[32,128,128]{2,1,0:T(8,128)(2,1)} %bitcast_bitcast_fusion), calls=%async_computation.1 | async-start | bytes 2097152 | tf_op jit(solution)/shard_map/all_to_all | solution.py:35
  221.5 77.8 %all-to-all-start.2 = ((bf16[128,16,256]{2,0,1:T(8,128)(2,1)}), bf16[128,16,256]{2,0,1:T(8,128)(2,1)S(1)}, u32[]{:S(2)}, u32[]{:S(2)}) async-start(bf16[128,16,256]{2,0,1:T(8,128)(2,1)} %copy.29), calls=%async_computation.2 | async-start | bytes 2097152 | tf_op jit(solution)/shard_map/all_to_all | solution.py:86
Sparse Core Ops, SparseCore 0:
  11.0 149.8 all-gather.2
  178.3 116.0 all-gather.4
where the time goes:
time: 312 us; the launch traced here: 311 us
  waiting for transfers between devices  171 us (55%)
  blocking collectives  38 us (12%)
  local copies, waits for them, and re-layouts  34.5 us (11%)
  starting transfers between devices  25.5 us (8%)
  matrix products  14.3 us (5%)
  between operations  14.1 us (5%)
  other arithmetic  13.1 us (4%)
    all_gather x1, waiting for transfers between devices, body(): lax.all_gather(gate_up_codes, 'local', axis=1, tiled=True)  77 us
    all_gather x1, waiting for transfers between devices, sent_together(): out, at, outs = (lax.all_gather(both, axis, axis=dim, tiled=True), 0, [])  66.2 us
    all_gather x1, blocking collectives, body(): lax.all_gather(gate_up_scales, 'local', axis=1, tiled=True)  38 us
    all_to_all x1, waiting for transfers between devices, sent_and_summed(): lax.all_to_all(pieces, axis, split_axis=0, concat_axis=0, tiled=True)  27.3 us
    mul x2, local copies, waits for them, and re-layouts, dequant(): weight = blocked * scales.astype(jnp.float32)[..., :, None, :]  23.9 us
    all_to_all x1, starting transfers between devices, from_everyone(): lax.all_to_all(jnp.broadcast_to(array[None], (length, *array.shape)), axi...  11.6 us
    convert_element_type x1, other arithmetic, dequant(): return weight.reshape(shape).astype(jnp.bfloat16)  10.6 us
    all_to_all x1, starting transfers between devices, sent_and_summed(): lax.all_to_all(pieces, axis, split_axis=0, concat_axis=0, tiled=True)  7.78 us
  transfers between devices with their start and end apart: 5, of which 3 were waited for; matrix products, arithmetic and copies ran while one was open for 16% of the time, Pallas kernels for 0%

commit v1 on v0

--- a/solution.py
+++ b/solution.py
@@ -5,6 +5,12 @@
 from jax.sharding import PartitionSpec as P
 
 BLOCK = 128
+
+
+def stack_and_merge(x, mesh_axis, dim):
+    parts = lax.all_gather(x, mesh_axis, axis=0, tiled=False)
+    whole = jnp.concatenate(parts, axis=dim)
+    return whole
 
 
 def from_everyone(array, axis):
@@ -58,7 +64,7 @@
     features = gather_directly(tokens, "node", 1)
     width = features.shape[1]
     all_codes, all_scales = (
-        lax.all_gather(gate_up_codes, "local", axis=1, tiled=True),
+        stack_and_merge(gate_up_codes, "local", 1),
         lax.all_gather(gate_up_scales, "local", axis=1, tiled=True),
     )
     w_gu = dequant(all_codes, all_scales)

time: 312 us -> 334 us (1.071)
  the two profiles are of different devices: /device:TPU:8 before, /device:TPU:2 now
where the time goes in v1:
time: 334 us; the launch traced here: 333 us
  waiting for transfers between devices  158 us (47%)
  local copies, waits for them, and re-layouts  63 us (19%)
  blocking collectives  41.2 us (12%)
  starting transfers between devices  26.5 us (8%)
  other arithmetic  15.8 us (5%)
  matrix products  14.3 us (4%)
  between operations  14.1 us (4%)
    all_gather x1, waiting for transfers between devices, sent_together(): out, at, outs = (lax.all_gather(both, axis, axis=dim, tiled=True), 0, [])  68.4 us
    all_gather x1, waiting for transfers between devices, stack_and_merge(): parts = lax.all_gather(x, mesh_axis, axis=0, tiled=False)  61.3 us
    all_gather x1, blocking collectives, body(): lax.all_gather(gate_up_scales, 'local', axis=1, tiled=True)  41.2 us
    convert_element_type x2, local copies, waits for them, and re-layouts, dequant(): codes.astype(jnp.float32)  28.6 us
    all_to_all x1, waiting for transfers between devices, sent_and_summed(): lax.all_to_all(pieces, axis, split_axis=0, concat_axis=0, tiled=True)  27.6 us
    mul x2, local copies, waits for them, and re-layouts, dequant(): weight = blocked * scales.astype(jnp.float32)[..., :, None, :]  23.9 us
    convert_element_type x1, other arithmetic, dequant(): return weight.reshape(shape).astype(jnp.bfloat16)  13.3 us
    all_to_all x1, starting transfers between devices, from_everyone(): lax.all_to_all(jnp.broadcast_to(array[None], (length, *array.shape)), axi...  11.9 us
  transfers between devices with their start and end apart: 5, of which 3 were waited for; matrix products, arithmetic and copies ran while one was open for 25% of the time, Pallas kernels for 0%

profile of v1, /device:TPU:2, one launch (start us, length us, event | category | flops | bytes accessed | tf_op | source)
XLA Modules:
  0.0 332.9 jit_solution(1886687241716291709)
XLA Ops:
  7.2 0.0 all-gather.6.cloned.1.call-start
  7.2 0.7 all-gather.6.cloned.1.call-update
  7.9 0.9 copy.27
  8.8 1.3 broadcast_in_dim.2
  10.0 11.9 %all-to-all-start = ((bf16[32,128,128]{1,2,0:T(8,128)(2,1)}), bf16[32,128,128]{1,2,0:T(8,128)(2,1)S(1)}, u32[]{:S(2)}, u32[]{:S(2)}) async-start(bf16[32,128,128]{1,2,0:T(8,128)(2,1)} %broadcast_in_dim.2), calls=%async_computation | async-start | bytes 2097152 | tf_op jit(solution)/shard_map/all_to_all | solution.py:18
  22.0 0.0 all-gather.4.cloned.1.call-start
  22.0 41.2 %all_gather.14 = bf16[2,32,448]{2,0,1:T(2,128)(2,1)S(1)} all-gather(bf16[2,2,448]{2,0,1:T(2,128)(2,1)S(1)} %copy.24), channel_id=1, replica_groups=mesh['node'=32,'local'=16] {'local'}, dimensions={1}, use_global_device_ids=true | all-gather | bytes 60928 | tf_op jit(solution)/shard_map/all_gather | solution.py:68
  63.3 0.2 copy.26
  63.5 7.8 %mul.45 = f32[2,32,128,448]{2,1,3,0:T(8,128)} broadcast(f32[2,32,448]{1,2,0:T(8,128)S(1)} %copy.26), dimensions={0,1,3} | broadcast | bytes 14794752 | tf_op jit(solution)/shard_map/mul | solution.py:57
  71.3 16.1 %mul.46 = f32[2,4096,448]{1,2,0:T(8,128)} reshape(f32[2,32,128,448]{2,1,3,0:T(8,128)} %mul.45) | data formatting | bytes 29360128 | tf_op jit(solution)/shard_map/mul | solution.py:57
  87.4 61.3 %all-gather.6.cloned.1.call-done = bf16[32,256,448]{1,2,0:T(8,128)(2,1)} async-done(((bf16[2,256,448]{1,2,0:T(8,128)(2,1)}), bf16[32,256,448]{1,2,0:T(8,128)(2,1)}) %all-gather.6.cloned.1.call-update) | async-done | bytes 7340048 | tf_op jit(solution)/shard_map/all_gather | solution.py:11
  148.7 12.6 %copy.40 = f32[16,2,256,448]{2,0,3,1:T(8,128)} copy(bf16[16,2,256,448]{2,3,1,0:T(8,128)(2,1)} %bitcast.64) | data formatting | bytes 22020096 | tf_op jit(solution)/shard_map/convert_element_type | solution.py:56
  161.2 16.0 %reshape.43 = f32[2,4096,448]{1,2,0:T(8,128)} reshape(f32[2,16,256,448]{2,1,3,0:T(8,128)} %bitcast.63) | data formatting | bytes 29360128 | tf_op jit(solution)/shard_map/convert_element_type | solution.py:56
  177.2 13.3 %multiply_convert_fusion = bf16[2,4096,448]{1,2,0:T(8,128)(2,1)} fusion(f32[2,4096,448]{1,2,0:T(8,128)} %reshape.43, f32[2,4096,448]{1,2,0:T(8,128)} %mul.46), kind=kLoop, calls=%fused_computation.2 | loop fusion | flops 7340032 | bytes 36700160 | tf_op jit(solution)/shard_map/convert_element_type | solution.py:58
  190.5 3.3 fusion.8
  193.8 0.9 copy-done
  194.7 1.8 fusion.12
  196.5 0.7 pad_maximum_fusion
  197.2 0.0 all-gather.4.cloned.1.call-update
  197.2 2.8 fusion.4
  200.0 2.8 fusion
  202.8 1.3 bitcast_bitcast_fusion
  204.1 9.0 %all-to-all-start.1 = ((bf16[32,128,128]{2,1,0:T(8,128)(2,1)}), bf16[32,128,128]{2,1,0:T(8,128)(2,1)S(1)}, u32[]{:S(2)}, u32[]{:S(2)}) async-start(bf16[32,128,128]{2,1,0:T(8,128)(2,1)} %bitcast_bitcast_fusion), calls=%async_computation.1 | async-start | bytes 2097152 | tf_op jit(solution)/shard_map/all_to_all | solution.py:41
  213.1 1.3 copy.31
  214.4 27.6 %all-to-all-done.1 = bf16[32,128,128]{2,1,0:T(8,128)(2,1)S(1)} async-done(((bf16[32,128,128]{2,1,0:T(8,128)(2,1)}), bf16[32,128,128]{2,1,0:T(8,128)(2,1)S(1)}, u32[]{:S(2)}, u32[]{:S(2)}) %all-to-all-start.1) | async-done | bytes 1048608 | tf_op jit(solution)/shard_map/all_to_all | solution.py:41
  242.0 5.5 %all-to-all-start.2 = ((bf16[128,16,256]{2,0,1:T(8,128)(2,1)}), bf16[128,16,256]{2,0,1:T(8,128)(2,1)S(1)}, u32[]{:S(2)}, u32[]{:S(2)}) async-start(bf16[128,16,256]{2,0,1:T(8,128)(2,1)} %copy.31), calls=%async_computation.2 | async-start | bytes 2097152 | tf_op jit(solution)/shard_map/all_to_all | solution.py:92
  247.5 0.8 reduce_sum.21
  248.3 68.4 %all-gather.4.cloned.1.call-done = bf16[2048,896]{0,1:T(8,128)(2,1)} async-done(((bf16[128,896]{0,1:T(8,128)(2,1)}), bf16[2048,896]{0,1:T(8,128)(2,1)}) %all-gather.4.cloned.1.call-update) | async-done | bytes 3670032 | tf_op jit(solution)/shard_map/all_gather | solution.py:47
  316.7 2.5 slice_bitcast_fusion.7
  319.2 2.2 copy_bitcast_fusion.1
  321.5 3.6 %convert_reduce_fusion = f32[896,256]{1,0:T(8,128)S(1)} fusion(bf16[16,128,448]{1,2,0:T(8,128)(2,1)S(1)} %get-tuple-element.8, bf16[16,128,448]{1,2,0:T(8,128)(2,1)} %get-tuple-element.9, bf16[128,16,256]{2,0,1:T(8,128)(2,1)S(1)} %all-to-all-done.2), kind=kOutput, calls=%fused_computation.1 | convolution fusion | flops 957644800 | bytes 5636096 | tf_op jit(solution)/shard_map/dot_general | solution.py:100
  325.1 1.0 broadcast_multiply_fusion
  (9 shorter events, 0.0 us)
Async XLA Ops:
  7.2 14.9 %copy-start.1 = (bf16[2,2,448]{2,1,0:T(2,128)(2,1)S(1)}, bf16[2,2,448]{2,1,0:T(2,128)(2,1)}, u32[]{:S(2)}) copy-start(bf16[2,2,448]{2,1,0:T(2,128)(2,1)} %param.6) | copy-start | bytes 10756
  7.2 141.5 %all-gather.6.cloned.1.call-start = ((), (), s32[]{:S(2)}) async-start(), calls=%async_computation.4 | async-start | bytes 7798784 | tf_op jit(solution)/shard_map/all_gather | solution.py:11
  10.0 180.5 %all-to-all-start = ((bf16[32,128,128]{1,2,0:T(8,128)(2,1)}), bf16[32,128,128]{1,2,0:T(8,128)(2,1)S(1)}, u32[]{:S(2)}, u32[]{:S(2)}) async-start(bf16[32,128,128]{1,2,0:T(8,128)(2,1)} %broadcast_in_dim.2), calls=%async_computation | async-start | bytes 2097152 | tf_op jit(solution)/shard_map/all_to_all | solution.py:18
  22.0 294.7 %all-gather.4.cloned.1.call-start = ((), (), s32[]{:S(2)}) async-start(), calls=%async_computation.3 | async-start | bytes 3899392 | tf_op jit(solution)/shard_map/all_gather | solution.py:47
  177.2 16.6 %copy-start.2 = (bf16[128,448]{0,1:T(8,128)(2,1)S(1)}, bf16[128,448]{0,1:T(8,128)(2,1)}, u32[]{:S(2)}) copy-start(bf16[128,448]{0,1:T(8,128)(2,1)} %param.7) | copy-start | bytes 344068
  190.5 4.2 %copy-start = (bf16[2,4096,448]{1,2,0:T(8,128)(2,1)S(1)}, bf16[2,4096,448]{1,2,0:T(8,128)(2,1)}, u32[]{:S(2)}) copy-start(bf16[2,4096,448]{1,2,0:T(8,128)(2,1)} %multiply_convert_fusion) | copy-start | bytes 22020100
  204.1 37.9 %all-to-all-start.1 = ((bf16[32,128,128]{2,1,0:T(8,128)(2,1)}), bf16[32,128,128]{2,1,0:T(8,128)(2,1)S(1)}, u32[]{:S(2)}, u32[]{:S(2)}) async-start(bf16[32,128,128]{2,1,0:T(8,128)(2,1)} %bitcast_bitcast_fusion), calls=%async_computation.1 | async-start | bytes 2097152 | tf_op jit(solution)/shard_map/all_to_all | solution.py:41
  242.0 79.5 %all-to-all-start.2 = ((bf16[128,16,256]{2,0,1:T(8,128)(2,1)}), bf16[128,16,256]{2,0,1:T(8,128)(2,1)S(1)}, u32[]{:S(2)}, u32[]{:S(2)}) async-start(bf16[128,16,256]{2,0,1:T(8,128)(2,1)} %copy.31), calls=%async_computation.2 | async-start | bytes 2097152 | tf_op jit(solution)/shard_map/all_to_all | solution.py:92
Sparse Core Ops, SparseCore 0:
  11.2 137.4 all-gather.5
  197.3 119.3 all-gather.3
